TPU v7x, 512 devices: a whole 4x4x16 slice. The times are simulated.
512 devices in a mesh: sec: 16 (over y, x_hi, core), op: 32 (over z, x_lo).
Axes of the slice: x: 4 (x_hi: 2, x_lo: 2; x = x_hi * 2 + x_lo), y: 4, z: 16, core: 2. Of those that a mesh axis runs over, the one named last changes fastest.
Arguments:
- wavefunction: bfloat16 [32, 256, 256], P('sec'), may hold values from -6 to 6
- diagonal: bfloat16 [32, 256, 256], P('sec'), may hold values from 1 to 4
- preconditioner: bfloat16 [32, 256, 256], P('sec'), may hold values from 0.25 to 1
- left_operator_blocks: bfloat16 [8192, 256, 256], P(('sec', 'op')), may hold values from -0.1875 to 0.1875
- right_operator_blocks: bfloat16 [8192, 256, 256], P(('sec', 'op')), may hold values from -0.375 to 0.375
- slot_source_sector: int32 [8192], P(('sec', 'op')), may hold values from 0 to 31
- slot_target_sector: int32 [8192], P(('sec', 'op')), may hold values from 0 to 1
- pair_count: int32 [512], P(('sec', 'op')), may hold values from 1 to 16, as said below
- left_dims: int32 [32], replicated, may hold values from 128 to 256, as said below
- right_dims: int32 [32], replicated, may hold values from 128 to 256, as said below
Outputs:
- correction: bfloat16 [32, 256, 256], P('sec')
- product_rows: float32 [32, 256, 256], P('sec', 'op')
- projected: float32 [3], replicated
Inputs may be any that keep to these rules, and one draw needn't show every extreme that they name: `pair_count`: slots below a device's count hold pairs, the rest are ignored; some device has all 16 slots live. `left_dims`: some sector uses all 256 rows. `right_dims`: some sector uses all 256 columns.
All inputs are finite; a program needn't handle non-finite values.
Results may differ from a plain program's by a relative error of at most 0.003.
Values may be sent and summed in bfloat16 or wider, within the bound.
No kernel may reach another device: no remote copies, remote signals or barrier semaphores. Data moves between devices by JAX's collectives and lax.ppermute only.
A program may use at most 64 MiB of HBM per device.

v0:
```python
import jax
import jax.numpy as jnp
from jax import lax
from jax.sharding import PartitionSpec as P


def block_mask(left_dims, right_dims, block_size):
    positions = jnp.arange(block_size, dtype=jnp.int32)
    return (positions[None, :, None] < left_dims[:, None, None]) & (
        positions[None, None, :] < right_dims[:, None, None]
    )


def gather_sources(own_vector):
    return lax.all_gather(own_vector, "sec", axis=0, tiled=True)


def reduce_dots(values):
    return lax.psum(values, "sec")


def pair_partial(
    sources,
    left_operator_blocks,
    right_operator_blocks,
    slot_source_sector,
    slot_target_sector,
    live_count,
    sector_count,
):
    block_size = sources.shape[1]
    zero_sum = jnp.zeros((sector_count, block_size, block_size), jnp.float32)

    def add_pair(slot_index, partial_value):
        source_block = lax.dynamic_index_in_dim(
            sources, slot_source_sector[slot_index], 0, keepdims=False
        )
        middle = jnp.dot(
            left_operator_blocks[slot_index], source_block, preferred_element_type=jnp.float32
        )
        contribution = jnp.dot(
            middle,
            right_operator_blocks[slot_index].astype(jnp.float32),
            precision=lax.Precision.HIGHEST,
            preferred_element_type=jnp.float32,
        )
        contribution = jnp.where(slot_index < live_count, contribution, 0.0)
        return partial_value.at[slot_target_sector[slot_index]].add(contribution)

    return lax.fori_loop(0, left_operator_blocks.shape[0], add_pair, zero_sum)


def sum_pairs(partial_value):
    return lax.psum(partial_value, "op")


def on_device(
    wavefunction,
    diagonal,
    preconditioner,
    left_operator_blocks,
    right_operator_blocks,
    slot_source_sector,
    slot_target_sector,
    pair_count,
    left_dims,
    right_dims,
):
    sector_count = wavefunction.shape[0]
    block_size = wavefunction.shape[1]
    op_devices = lax.axis_size("op")
    share_rows = block_size // op_devices
    first_sector = lax.axis_index("sec") * sector_count
    row_start = lax.axis_index("op") * share_rows
    entries = float(left_dims.shape[0] * block_size * block_size)
    own_mask = block_mask(
        lax.dynamic_slice_in_dim(left_dims, first_sector, sector_count),
        lax.dynamic_slice_in_dim(right_dims, first_sector, sector_count),
        block_size,
    )
    live_count = pair_count[0]
    own_vector = jnp.where(own_mask, wavefunction, jnp.zeros_like(wavefunction))
    diag_view = diagonal.astype(jnp.float32)
    scale_view = preconditioner.astype(jnp.float32)
    vector_view = own_vector.astype(jnp.float32)

    def apply_operator(sources, field_view):
        partial_value = pair_partial(
            sources,
            left_operator_blocks,
            right_operator_blocks,
            slot_source_sector,
            slot_target_sector,
            live_count,
            sector_count,
        )
        return jnp.where(own_mask, diag_view * field_view + sum_pairs(partial_value), 0.0)

    sigma_first = apply_operator(gather_sources(own_vector), vector_view)
    norm_vector, correlation = reduce_dots(
        (jnp.sum(vector_view * vector_view), jnp.sum(vector_view * sigma_first))
    )
    rayleigh = correlation / norm_vector
    residual = sigma_first - rayleigh * vector_view
    scaled = scale_view * residual
    along_vector = reduce_dots((jnp.sum(vector_view * scaled),))[0]
    orthogonal = scaled - along_vector / norm_vector * vector_view
    square_norm = reduce_dots((jnp.sum(orthogonal * orthogonal),))[0]
    corr_view = (orthogonal * lax.rsqrt(square_norm / entries + 1e-06)).astype(jnp.bfloat16)
    next_sources = gather_sources(corr_view)
    corr_float = corr_view.astype(jnp.float32)
    sigma_second = apply_operator(next_sources, corr_float)
    cross_term, self_term = reduce_dots(
        (jnp.sum(vector_view * sigma_second), jnp.sum(corr_float * sigma_second))
    )
    projected = jnp.stack(
        [rayleigh, cross_term * lax.rsqrt(norm_vector * entries), self_term / entries]
    )
    product_rows = lax.dynamic_slice_in_dim(sigma_second, row_start, share_rows, 1)
    return (corr_view, product_rows, projected)


def solution(mesh):
    in_specs = (
        P("sec", None, None),
        P("sec", None, None),
        P("sec", None, None),
        P(("sec", "op"), None, None),
        P(("sec", "op"), None, None),
        P(("sec", "op")),
        P(("sec", "op")),
        P(("sec", "op")),
        P(),
        P(),
    )
    out_specs = (P("sec", None, None), P("sec", "op", None), P())
    return jax.shard_map(
        on_device, mesh=mesh, in_specs=in_specs, out_specs=out_specs, check_vma=False
    )
```

profile of v0, /device:TPU:1, one launch (start us, length us, event | category | flops | bytes accessed | tf_op | source)
XLA Modules:
  0.0 1174.2 jit_solution(14956797437552450582)
XLA Ops:
  8.8 1.8 and_select_fusion.2
  10.6 77.2 %all-gather.3.cloned.1.call-done = bf16[32,256,256]{2,1,0:T(8,128)(2,1)} async-done(((bf16[2,256,256]{2,1,0:T(8,128)(2,1)}), bf16[32,256,256]{2,1,0:T(8,128)(2,1)}) %all-gather.3.cloned.1.call-update) | async-done | bytes 4194320 | tf_op jit(solution)/shard_map/all_gather | solution.py:15
  87.9 182.8 %while.28 = (s32[]{:T(128)}, f32[2,256,256]{2,1,0:T(8,128)S(1)}, s32[16]{0:T(128)}, s32[]{:T(128)}, bf16[16,256,256]{2,1,0:T(8,128)(2,1)}, /*index=5*/s32[16]{0:...) while((s32[]{:T(128)}, f32[2,256,256]{2,1,0:T(8,128)S(1)}, ...), condition=%wide.region_2.3_spmd, body=%wide.region_0.2_spmd.sunk | while | flops 235077664 | bytes 1444100 | solution.py:50
  87.9 1.3 dynamic_slice.122
  92.3 1.2 dynamic_slice.121
  95.5 1.4 and_reduce_fusion.4
  97.5 1.8 fusion.55
  106.9 1.4 and_reduce_fusion.4
  108.9 1.8 fusion.55
  118.3 1.4 and_reduce_fusion.4
  120.3 1.8 fusion.55
  129.7 1.4 and_reduce_fusion.4
  131.8 1.8 fusion.55
  141.2 1.4 and_reduce_fusion.4
  143.2 1.8 fusion.55
  152.6 1.4 and_reduce_fusion.4
  154.6 1.8 fusion.55
  164.0 1.4 and_reduce_fusion.4
  166.0 1.8 fusion.55
  175.4 1.4 and_reduce_fusion.4
  177.4 1.8 fusion.55
  186.8 1.4 and_reduce_fusion.4
  188.9 1.8 fusion.55
  198.3 1.4 and_reduce_fusion.4
  200.3 1.8 fusion.55
  209.7 1.4 and_reduce_fusion.4
  211.7 1.8 fusion.55
  221.1 1.4 and_reduce_fusion.4
  223.1 1.8 fusion.55
  232.5 1.4 and_reduce_fusion.4
  234.5 1.8 fusion.55
  243.9 1.4 and_reduce_fusion.4
  246.0 1.8 fusion.55
  255.3 1.4 and_reduce_fusion.4
  257.4 1.8 fusion.55
  266.8 1.4 and_reduce_fusion.4
  268.8 1.8 fusion.55
  271.5 241.5 %all-reduce.5.cloned.1.call-done = f32[2,256,256]{2,1,0:T(8,128)} async-done(((f32[2,256,256]{2,1,0:T(8,128)}), f32[2,256,256]{2,1,0:T(8,128)}) %all-reduce.5.cloned.1.call-update) | async-done | bytes 524304 | tf_op jit(solution)/shard_map/psum | solution.py:54
  513.0 2.0 fusion.30
  515.1 55.5 %all-reduce.1 = (f32[]{:T(128)}, f32[]{:T(128)}) all-reduce(f32[]{:T(128)} %get-tuple-element.330, f32[]{:T(128)} %get-tuple-element.329), channel_id=1, replica_groups=mesh['sec'=16,'op'=32] {'sec'}, use_global_device_ids=true, to_apply=%region_5.6 | all-reduce | flops 2 | bytes 16 | tf_op jit(solution)/shard_map/psum | solution.py:19
  571.9 2.0 fusion.33
  574.0 33.8 %psum.59 = f32[]{:T(128)} all-reduce(f32[]{:T(128)} %fusion.33), channel_id=1, replica_groups=mesh['sec'=16,'op'=32] {'sec'}, use_global_device_ids=true, to_apply=%region_9.10 | all-reduce | flops 1 | bytes 8 | tf_op jit(solution)/shard_map/psum | solution.py:19
  610.1 33.8 %psum.60 = f32[]{:T(128)} all-reduce(f32[]{:T(128)} %multiply_reduce_fusion), channel_id=1, replica_groups=mesh['sec'=16,'op'=32] {'sec'}, use_global_device_ids=true, to_apply=%region_11.12 | all-reduce | flops 1 | bytes 8 | tf_op jit(solution)/shard_map/psum | solution.py:19
  645.7 64.4 %all-gather.5.cloned.1.call-done = bf16[32,256,256]{2,1,0:T(8,128)(2,1)} async-done(((bf16[2,256,256]{2,1,0:T(8,128)(2,1)}), bf16[32,256,256]{2,1,0:T(8,128)(2,1)}) %all-gather.5.cloned.1.call-update) | async-done | bytes 4194320 | tf_op jit(solution)/shard_map/all_gather | solution.py:15
  710.2 155.1 %while.29 = (s32[]{:T(128)}, f32[2,256,256]{2,1,0:T(8,128)S(1)}, s32[16]{0:T(128)S(1)}, s32[]{:T(128)}, bf16[16,256,256]{2,1,0:T(8,128)(2,1)}, /*index=5*/s32[16...) while((s32[]{:T(128)}, f32[2,256,256]{2,1,0:T(8,128)S(1)}, ...), condition=%wide.region_14.15_spmd, body=%wide.region_12.14_spmd.sunk | while | flops 235077664 | bytes 1444100 | solution.py:50
  718.0 1.9 fusion.61
  727.7 1.9 fusion.61
  737.4 1.9 fusion.61
  747.1 1.9 fusion.61
  756.8 1.9 fusion.61
  766.5 1.9 fusion.61
  776.2 1.9 fusion.61
  785.9 1.9 fusion.61
  795.5 1.9 fusion.61
  805.2 1.9 fusion.61
  814.9 1.9 fusion.61
  824.6 1.9 fusion.61
  834.3 1.9 fusion.61
  844.0 1.9 fusion.61
  853.7 1.9 fusion.61
  863.4 1.9 fusion.61
  866.8 240.9 %all-reduce.7.cloned.1.call-done = f32[2,256,256]{2,1,0:T(8,128)} async-done(((f32[2,256,256]{2,1,0:T(8,128)}), f32[2,256,256]{2,1,0:T(8,128)}) %all-reduce.7.cloned.1.call-update) | async-done | bytes 524304 | tf_op jit(solution)/shard_map/psum | solution.py:54
  1107.7 2.0 fusion.35
  1109.7 55.5 %all-reduce = (f32[]{:T(128)}, f32[]{:T(128)}) all-reduce(f32[]{:T(128)} %get-tuple-element.328, f32[]{:T(128)} %get-tuple-element.327), channel_id=1, replica_groups=mesh['sec'=16,'op'=32] {'sec'}, use_global_device_ids=true, to_apply=%region_19.20 | all-reduce | flops 2 | bytes 16 | tf_op jit(solution)/shard_map/psum | solution.py:19
  (147 shorter events, 114.2 us)
Async XLA Ops:
  7.2 80.6 %all-gather.3.cloned.1.call-start = ((), (), s32[]{:S(2)}) async-start(), calls=%async_computation | async-start | bytes 4456448 | tf_op jit(solution)/shard_map/all_gather | solution.py:15
  10.6 502.5 %all-reduce.5.cloned.1.call-start = ((), (), s32[]{:S(2)}) async-start(), calls=%async_computation.1 | async-start | bytes 1048576 | tf_op jit(solution)/shard_map/psum | solution.py:54
  87.8 425.2 %copy-start.2 = (bf16[2,256,256]{2,1,0:T(8,128)(2,1)S(1)}, bf16[2,256,256]{2,1,0:T(8,128)(2,1)}, u32[]{:S(2)}) copy-start(bf16[2,256,256]{2,1,0:T(8,128)(2,1)} %param.18) | copy-start | bytes 786436
  87.8 425.2 %copy-start.4 = (bf16[2,256,256]{2,1,0:T(8,128)(2,1)S(1)}, bf16[2,256,256]{2,1,0:T(8,128)(2,1)}, u32[]{:S(2)}) copy-start(bf16[2,256,256]{2,1,0:T(8,128)(2,1)} %param.19) | copy-start | bytes 786436
  87.9 484.1 %copy-start.6 = (bf16[2,256,256]{2,1,0:T(8,128)(2,1)S(1)}, bf16[2,256,256]{2,1,0:T(8,128)(2,1)}, u32[]{:S(2)}) copy-start(bf16[2,256,256]{2,1,0:T(8,128)(2,1)} %param.20) | copy-start | bytes 786436
  270.6 0.8 copy-start.1
  271.5 438.6 %all-gather.5.cloned.1.call-start = ((), (), s32[]{:S(2)}) async-start(), calls=%async_computation.2 | async-start | bytes 4456448 | tf_op jit(solution)/shard_map/all_gather | solution.py:15
  513.0 96.0 %copy-start.3 = (f32[2,256,256]{2,1,0:T(8,128)S(1)}, f32[2,256,256]{2,1,0:T(8,128)}, u32[]{:S(2)}) copy-start(f32[2,256,256]{2,1,0:T(8,128)} %all-reduce.5.cloned.1.call-done) | copy-start | bytes 1572868
  574.0 136.2 %copy-start.7 = (s32[3]{0:T(128)S(1)}, s32[3]{0:T(128)}, u32[]{:S(2)}) copy-start(s32[3]{0:T(128)} %get-tuple-element.570) | copy-start | bytes 40
  574.0 136.2 %copy-start.8 = (s32[16]{0:T(128)S(1)}, s32[16]{0:T(128)}, u32[]{:S(2)}) copy-start(s32[16]{0:T(128)} %get-tuple-element.571) | copy-start | bytes 196
  574.0 136.2 %copy-start.9 = (s32[16]{0:T(128)S(1)}, s32[16]{0:T(128)}, u32[]{:S(2)}) copy-start(s32[16]{0:T(128)} %get-tuple-element.572) | copy-start | bytes 196
  645.6 462.1 %all-reduce.7.cloned.1.call-start = ((), (), s32[]{:S(2)}) async-start(), calls=%async_computation.3 | async-start | bytes 1048576 | tf_op jit(solution)/shard_map/psum | solution.py:54
  710.2 397.5 %copy-start.5 = (bf16[2,256,256]{2,1,0:T(8,128)(2,1)S(1)}, bf16[2,256,256]{2,1,0:T(8,128)(2,1)}, u32[]{:S(2)}) copy-start(bf16[2,256,256]{2,1,0:T(8,128)(2,1)} %multiply_convert_fusion) | copy-start | bytes 786436
  865.3 0.8 copy-start
Sparse Core Ops, SparseCore 0:
  11.9 75.8 all-gather.2
  271.6 241.3 all-reduce.4
  645.7 64.3 all-gather.4
  866.2 241.3 all-reduce.6
where the time goes:
time: 1180 us; the launch traced here: 1170 us
  waiting for transfers between devices  624 us (53%)
  blocking collectives  179 us (15%)
  loops' own time  147 us (12%)
  matrix products  96.2 us (8%)
  local copies, waits for them, and re-layouts  64.2 us (5%)
  other arithmetic  45.2 us (4%)
  between operations  19.2 us (2%)
    psum x2, waiting for transfers between devices, sum_pairs(): return lax.psum(partial_value, 'op')  482 us
    psum x4, blocking collectives, reduce_dots(): return lax.psum(values, 'sec')  179 us
    another operation x2, loops' own time, pair_partial(): return lax.fori_loop(0, left_operator_blocks.shape[0], add_pair, zero_sum)  147 us
    all_gather x2, waiting for transfers between devices, gather_sources(): return lax.all_gather(own_vector, 'sec', axis=0, tiled=True)  142 us
    dot_general x32, matrix products, add_pair(): jnp.dot(middle, right_operator_blocks[slot_index].astype(jnp.float32), pr...  59.3 us
    dot_general x32, matrix products, add_pair(): jnp.dot(left_operator_blocks[slot_index], source_block, preferred_element...  36.9 us
    another operation x32, other arithmetic  34.6 us
    dynamic_slice x32, local copies, waits for them, and re-layouts, add_pair(): return partial_value.at[slot_target_sector[slot_index]].add(contribution)  30.6 us
  transfers between devices with their start and end apart: 4, of which 4 were waited for; matrix products, arithmetic and copies ran while one was open for 0% of the time, Pallas kernels for 0%

commit v1 on v0

--- a/solution.py
+++ b/solution.py
@@ -12,7 +12,9 @@
 
 
 def gather_sources(own_vector):
-    return lax.all_gather(own_vector, "sec", axis=0, tiled=True)
+    return jnp.concatenate(
+        lax.all_to_all(jnp.stack([own_vector] * lax.axis_size("sec")), "sec", 0, 0), axis=0
+    )
 
 
 def reduce_dots(values):

time: 1180 us -> 1120 us (0.949)
  waiting for transfers between devices: 624 us -> 583 us
  local copies, waits for them, and re-layouts: 64.2 us -> 47 us
  starting transfers between devices: 0.16 us -> 16.2 us
  other arithmetic: 45.2 us -> 32.4 us
    all_gather x2 -> x0, waiting for transfers between devices: 142 us -> none  [gather_sources(): return lax.all_gather(own_vector, 'sec', axis=0, tiled=True)]
    all_to_all x0 -> x2, waiting for transfers between devices: none -> 102 us  [gather_sources(): lax.all_to_all(jnp.stack([own_vector] * lax.axis_size('sec')), 'sec', 0, 0)]
    all_to_all x0 -> x2, starting transfers between devices: none -> 16.1 us  [gather_sources(): lax.all_to_all(jnp.stack([own_vector] * lax.axis_size('sec')), 'sec', 0, 0)]
where the time goes in v1:
time: 1120 us; the launch traced here: 1110 us
  waiting for transfers between devices  583 us (52%)
  blocking collectives  179 us (16%)
  loops' own time  143 us (13%)
  matrix products  94.9 us (8%)
  local copies, waits for them, and re-layouts  47 us (4%)
  other arithmetic  32.4 us (3%)
  between operations  19.5 us (2%)
  starting transfers between devices  16.2 us (1%)
    psum x2, waiting for transfers between devices, sum_pairs(): return lax.psum(partial_value, 'op')  481 us
    psum x4, blocking collectives, reduce_dots(): return lax.psum(values, 'sec')  179 us
    another operation x2, loops' own time, pair_partial(): return lax.fori_loop(0, left_operator_blocks.shape[0], add_pair, zero_sum)  143 us
    all_to_all x2, waiting for transfers between devices, gather_sources(): lax.all_to_all(jnp.stack([own_vector] * lax.axis_size('sec')), 'sec', 0, 0)  102 us
    dot_general x32, matrix products, add_pair(): jnp.dot(middle, right_operator_blocks[slot_index].astype(jnp.float32), pr...  57.9 us
    dot_general x32, matrix products, add_pair(): jnp.dot(left_operator_blocks[slot_index], source_block, preferred_element...  36.9 us
    another operation x32, other arithmetic  23.2 us
  transfers between devices with their start and end apart: 4, of which 4 were waited for; matrix products, arithmetic and copies ran while one was open for 0% of the time, Pallas kernels for 0%

profile of v1, /device:TPU:1, one launch (start us, length us, event | category | flops | bytes accessed | tf_op | source)
XLA Modules:
  0.0 1114.2 jit_solution(12039212435376230666)
XLA Ops:
  9.8 2.4 stack.12
  12.3 11.2 %all-to-all-start = ((bf16[16,2,256,256]{3,2,1,0:T(8,128)(2,1)}), bf16[16,2,256,256]{3,2,1,0:T(8,128)(2,1)}, u32[]{:S(2)}, u32[]{:S(2)}) async-start(bf16[16,2,256,256]{3,2,1,0:T(8,128)(2,1)} %stack.12), calls=%async_computation | async-start | bytes 8388608 | tf_op jit(solution)/shard_map/all_to_all | solution.py:16
  23.5 51.0 %all-to-all-done = bf16[16,2,256,256]{3,2,1,0:T(8,128)(2,1)} async-done(((bf16[16,2,256,256]{3,2,1,0:T(8,128)(2,1)}), bf16[16,2,256,256]{3,2,1,0:T(8,128)(2,1)}, u32[]{:S(2)}, u32[]{:S(2)}) %all-to-all-start) | async-done | bytes 4194336 | tf_op jit(solution)/shard_map/all_to_all | solution.py:16
  74.6 151.0 %while.28 = (s32[]{:T(128)}, f32[2,256,256]{2,1,0:T(8,128)S(1)}, s32[16]{0:T(128)S(1)}, s32[]{:T(128)}, bf16[16,256,256]{2,1,0:T(8,128)(2,1)}, /*index=5*/s32[16...) while((s32[]{:T(128)}, f32[2,256,256]{2,1,0:T(8,128)S(1)}, ...), condition=%wide.region_2.3_spmd, body=%wide.region_0.2_spmd.sunk | while | flops 235077664 | bytes 1444100 | solution.py:52
  77.1 1.2 fusion.54
  82.2 1.8 fusion.55
  91.7 1.8 fusion.55
  101.1 1.8 fusion.55
  110.5 1.8 fusion.55
  120.0 1.8 fusion.55
  129.4 1.8 fusion.55
  138.9 1.8 fusion.55
  148.3 1.8 fusion.55
  157.7 1.8 fusion.55
  167.2 1.8 fusion.55
  176.6 1.8 fusion.55
  186.1 1.8 fusion.55
  195.5 1.8 fusion.55
  204.9 1.8 fusion.55
  214.4 1.8 fusion.55
  223.8 1.8 fusion.55
  226.5 242.2 %all-reduce.5.cloned.1.call-done = f32[2,256,256]{2,1,0:T(8,128)} async-done(((f32[2,256,256]{2,1,0:T(8,128)}), f32[2,256,256]{2,1,0:T(8,128)}) %all-reduce.5.cloned.1.call-update) | async-done | bytes 524304 | tf_op jit(solution)/shard_map/psum | solution.py:56
  468.7 2.0 fusion.30
  470.7 55.5 %all-reduce.1 = (f32[]{:T(128)}, f32[]{:T(128)}) all-reduce(f32[]{:T(128)} %get-tuple-element.330, f32[]{:T(128)} %get-tuple-element.329), channel_id=1, replica_groups=mesh['sec'=16,'op'=32] {'sec'}, use_global_device_ids=true, to_apply=%region_5.6 | all-reduce | flops 2 | bytes 16 | tf_op jit(solution)/shard_map/psum | solution.py:21
  527.6 2.0 fusion.33
  529.6 33.8 %psum.59 = f32[]{:T(128)} all-reduce(f32[]{:T(128)} %fusion.33), channel_id=1, replica_groups=mesh['sec'=16,'op'=32] {'sec'}, use_global_device_ids=true, to_apply=%region_9.10 | all-reduce | flops 1 | bytes 8 | tf_op jit(solution)/shard_map/psum | solution.py:21
  565.7 33.8 %psum.60 = f32[]{:T(128)} all-reduce(f32[]{:T(128)} %multiply_reduce_fusion), channel_id=1, replica_groups=mesh['sec'=16,'op'=32] {'sec'}, use_global_device_ids=true, to_apply=%region_11.12 | all-reduce | flops 1 | bytes 8 | tf_op jit(solution)/shard_map/psum | solution.py:21
  600.5 2.4 stack.13
  603.0 4.9 all-to-all-start.1
  607.9 51.0 %all-to-all-done.1 = bf16[16,2,256,256]{3,2,1,0:T(8,128)(2,1)} async-done(((bf16[16,2,256,256]{3,2,1,0:T(8,128)(2,1)}), bf16[16,2,256,256]{3,2,1,0:T(8,128)(2,1)}, u32[]{:S(2)}, u32[]{:S(2)}) %all-to-all-start.1) | async-done | bytes 4194336 | tf_op jit(solution)/shard_map/all_to_all | solution.py:16
  658.9 148.3 %while.29 = (s32[]{:T(128)}, f32[2,256,256]{2,1,0:T(8,128)S(1)}, s32[16]{0:T(128)S(1)}, s32[]{:T(128)}, bf16[16,256,256]{2,1,0:T(8,128)(2,1)}, /*index=5*/s32[16...) while((s32[]{:T(128)}, f32[2,256,256]{2,1,0:T(8,128)S(1)}, ...), condition=%wide.region_14.15_spmd, body=%wide.region_12.14_spmd.sunk | while | flops 235077664 | bytes 1444100 | solution.py:52
  666.4 1.8 fusion.61
  670.7 1.2 fusion.60
  675.7 1.8 fusion.61
  679.9 1.2 fusion.60
  684.9 1.8 fusion.61
  689.2 1.2 fusion.60
  694.2 1.8 fusion.61
  698.5 1.2 fusion.60
  703.5 1.8 fusion.61
  707.7 1.2 fusion.60
  712.8 1.8 fusion.61
  717.0 1.2 fusion.60
  722.0 1.8 fusion.61
  726.3 1.2 fusion.60
  731.3 1.8 fusion.61
  735.6 1.2 fusion.60
  740.6 1.8 fusion.61
  744.8 1.2 fusion.60
  749.8 1.8 fusion.61
  754.1 1.2 fusion.60
  759.1 1.8 fusion.61
  763.4 1.2 fusion.60
  768.4 1.8 fusion.61
  777.7 1.8 fusion.61
  781.9 1.2 fusion.60
  786.9 1.8 fusion.61
  791.2 1.2 fusion.60
  796.2 1.8 fusion.61
  800.5 1.2 fusion.60
  805.5 1.8 fusion.61
  808.8 238.6 %all-reduce.7.cloned.1.call-done = f32[2,256,256]{2,1,0:T(8,128)} async-done(((f32[2,256,256]{2,1,0:T(8,128)}), f32[2,256,256]{2,1,0:T(8,128)}) %all-reduce.7.cloned.1.call-update) | async-done | bytes 524304 | tf_op jit(solution)/shard_map/psum | solution.py:56
  1047.4 2.0 fusion.35
  1049.4 55.5 %all-reduce = (f32[]{:T(128)}, f32[]{:T(128)}) all-reduce(f32[]{:T(128)} %get-tuple-element.328, f32[]{:T(128)} %get-tuple-element.327), channel_id=1, replica_groups=mesh['sec'=16,'op'=32] {'sec'}, use_global_device_ids=true, to_apply=%region_19.20 | all-reduce | flops 2 | bytes 16 | tf_op jit(solution)/shard_map/psum | solution.py:21
  (147 shorter events, 88.1 us)
Async XLA Ops:
  12.3 62.3 %copy-start.7 = (s32[3]{0:T(128)S(1)}, s32[3]{0:T(128)}, u32[]{:S(2)}) copy-start(s32[3]{0:T(128)} %constant.174.clone.1) | copy-start | bytes 40
  12.3 62.3 %copy-start.8 = (s32[16]{0:T(128)S(1)}, s32[16]{0:T(128)}, u32[]{:S(2)}) copy-start(s32[16]{0:T(128)} %param.24) | copy-start | bytes 196
  12.3 62.3 %copy-start.9 = (s32[16]{0:T(128)S(1)}, s32[16]{0:T(128)}, u32[]{:S(2)}) copy-start(s32[16]{0:T(128)} %param.23) | copy-start | bytes 196
  12.3 62.2 %all-to-all-start = ((bf16[16,2,256,256]{3,2,1,0:T(8,128)(2,1)}), bf16[16,2,256,256]{3,2,1,0:T(8,128)(2,1)}, u32[]{:S(2)}, u32[]{:S(2)}) async-start(bf16[16,2,256,256]{3,2,1,0:T(8,128)(2,1)} %stack.12), calls=%async_computation | async-start | bytes 8388608 | tf_op jit(solution)/shard_map/all_to_all | solution.py:16
  23.5 445.2 %all-reduce.5.cloned.1.call-start = ((), (), s32[]{:S(2)}) async-start(), calls=%async_computation.2 | async-start | bytes 1048576 | tf_op jit(solution)/shard_map/psum | solution.py:56
  74.6 394.1 %copy-start.2 = (bf16[2,256,256]{2,1,0:T(8,128)(2,1)S(1)}, bf16[2,256,256]{2,1,0:T(8,128)(2,1)}, u32[]{:S(2)}) copy-start(bf16[2,256,256]{2,1,0:T(8,128)(2,1)} %param.18) | copy-start | bytes 786436
  74.6 394.1 %copy-start.4 = (bf16[2,256,256]{2,1,0:T(8,128)(2,1)S(1)}, bf16[2,256,256]{2,1,0:T(8,128)(2,1)}, u32[]{:S(2)}) copy-start(bf16[2,256,256]{2,1,0:T(8,128)(2,1)} %param.19) | copy-start | bytes 786436
  74.6 453.0 %copy-start.6 = (bf16[2,256,256]{2,1,0:T(8,128)(2,1)S(1)}, bf16[2,256,256]{2,1,0:T(8,128)(2,1)}, u32[]{:S(2)}) copy-start(bf16[2,256,256]{2,1,0:T(8,128)(2,1)} %param.20) | copy-start | bytes 786436
  225.7 0.8 copy-start.1
  468.7 96.0 %copy-start.3 = (f32[2,256,256]{2,1,0:T(8,128)S(1)}, f32[2,256,256]{2,1,0:T(8,128)}, u32[]{:S(2)}) copy-start(f32[2,256,256]{2,1,0:T(8,128)} %all-reduce.5.cloned.1.call-done) | copy-start | bytes 1572868
  600.5 446.9 %copy-start.5 = (bf16[2,256,256]{2,1,0:T(8,128)(2,1)}, bf16[2,256,256]{2,1,0:T(8,128)(2,1)S(1)}, u32[]{:S(2)}) copy-start(bf16[2,256,256]{2,1,0:T(8,128)(2,1)S(1)} %multiply_convert_fusion) | copy-start | bytes 786436
  603.0 55.9 %all-to-all-start.1 = ((bf16[16,2,256,256]{3,2,1,0:T(8,128)(2,1)}), bf16[16,2,256,256]{3,2,1,0:T(8,128)(2,1)}, u32[]{:S(2)}, u32[]{:S(2)}) async-start(bf16[16,2,256,256]{3,2,1,0:T(8,128)(2,1)} %stack.13), calls=%async_computation.1 | async-start | bytes 8388608 | tf_op jit(solution)/shard_map/all_to_all | solution.py:16
  607.9 439.5 %all-reduce.7.cloned.1.call-start = ((), (), s32[]{:S(2)}) async-start(), calls=%async_computation.3 | async-start | bytes 1048576 | tf_op jit(solution)/shard_map/psum | solution.py:56
  807.3 0.8 copy-start
Sparse Core Ops, SparseCore 0:
  226.6 241.9 all-reduce.4
  808.2 239.1 all-reduce.6
